TPU v7x, 32 devices: a whole 2x2x4 slice. The times are simulated.
32 devices in a mesh: groups: 2 (over x), ctx: 16 (over z, y, core).
Axes of the slice: x: 2, y: 2, z: 4, core: 2. Of those that a mesh axis runs over, the one named last changes fastest.
Arguments:
- query: bfloat16 [8192, 1024], P(('groups', 'ctx')), parts along dimension 0, may hold values from -130 to 130, as said below
- key: bfloat16 [8192, 1024], P(('groups', 'ctx')), parts along dimension 0, may hold values from -4.5 to 4.5
- value: bfloat16 [8192, 1024], P(('groups', 'ctx')), parts along dimension 0, may hold values from -6 to 6
- cotangent: bfloat16 [8192, 1024], P(('groups', 'ctx')), parts along dimension 0, may hold values from -6 to 6
- global_ids: int32 [4], P('groups'), parts along dimension 0, may hold values from 0 to 63
- rand_owner: int32 [128, 6], P('groups'), parts along dimension 0, may hold values from 0 to 15, all different within a row; in each aligned block of 4 rows (0 to 3, 4 to 7, ...) at most 2 rows name the same one
- rand_local: int32 [128, 6], P('groups'), parts along dimension 0, may hold values from 0 to 3
Outputs:
- attended: bfloat16 [8192, 1024], P(('groups', 'ctx')), parts along dimension 0
- grad_query: bfloat16 [8192, 1024], P(('groups', 'ctx')), parts along dimension 0
- grad_key: bfloat16 [8192, 1024], P(('groups', 'ctx')), parts along dimension 0
- grad_value: bfloat16 [8192, 1024], P(('groups', 'ctx')), parts along dimension 0
There are 2 independent parts, one for each index of `groups`. A program takes and returns all parts, laid end to end along the dimension named above; each array names one. Nothing has to cross between parts.
Inputs may be any that keep to these rules, and one draw needn't show every extreme that they name: query and key are drawn together. `rand_owner`: each row names 6 different devices. In the 4 rows of one device no device is named more than 2 times, and in some device's rows some device is named exactly 2 times.
All inputs are finite; a program needn't handle non-finite values.
Results may differ from a plain program's by a relative error of at most 0.017.
Values may be sent and summed in bfloat16 or wider, within the bound.
A program may use at most 192 MiB of HBM per device.

v0:
```python
import jax
import jax.numpy as jnp
from jax import lax
from jax.sharding import PartitionSpec as P

HEAD_DIM = 64
GROUP_HEADS = 8
BLOCK = 64
GLOBALS = 2
ROUNDS = 3
NEG_FILL = -1e30


def padded_2(block, sides, width):
    for axis, dim in sides:
        count = lax.axis_size(axis)
        forward = [(i, i + 1) for i in range(count - 1)]
        backward = [(target, source) for source, target in forward]
        low = lax.ppermute(
            lax.slice_in_dim(block, block.shape[dim] - width, None, axis=dim), axis, forward
        )
        high = lax.ppermute(lax.slice_in_dim(block, 0, width, axis=dim), axis, backward)
        block = jnp.concatenate([low, block, high], axis=dim)
    return block


def broadcast(array, axis, root):
    mine = lax.axis_index(axis) == root
    return lax.psum(jnp.where(mine, array, jnp.zeros_like(array)), axis)


def request_ranks(owners, device_count):
    onehot = (owners[:, :, None] == jnp.arange(device_count, dtype=jnp.int32)).astype(jnp.int32)
    before = jnp.cumsum(onehot, axis=1) - onehot
    return jnp.sum(before * onehot, axis=2)


def per_device(query, key, value, cotangent, global_ids, rand_owner, rand_local):
    tok_count, features = query.shape
    blocks = tok_count // BLOCK
    head_count = features // HEAD_DIM
    groups = head_count // GROUP_HEADS
    group_width = GROUP_HEADS * HEAD_DIM
    device_count = lax.axis_size("ctx")
    my_index = lax.axis_index("ctx")
    pick_count = groups * ROUNDS
    slot_count = max(2, (pick_count * blocks + device_count - 1) // device_count)
    score_scale = HEAD_DIM ** (-0.5)
    key_kinds = 3 + GLOBALS + ROUNDS
    key_span = key_kinds * BLOCK
    kv_local = jnp.stack(
        (key.reshape(blocks, BLOCK, features), value.reshape(blocks, BLOCK, features)), axis=2
    )
    padded = padded_2(kv_local, (("ctx", 0),), 1)
    glob_list = []
    for glob_index in range(GLOBALS):
        root_dev = global_ids[glob_index] // blocks
        local_block = global_ids[glob_index] % blocks
        block_kv = lax.dynamic_index_in_dim(kv_local, local_block, 0, keepdims=False)
        glob_list.append(broadcast(block_kv, "ctx", root_dev))
    glob_kv = jnp.stack(glob_list)
    owners_all = rand_owner.reshape(device_count, blocks * pick_count)
    locals_all = rand_local.reshape(device_count, blocks * pick_count)
    ranks_all = request_ranks(owners_all, device_count)
    my_owner = lax.dynamic_index_in_dim(owners_all, my_index, 0, keepdims=False)
    my_rank = lax.dynamic_index_in_dim(ranks_all, my_index, 0, keepdims=False)
    fetch_index = my_owner * slot_count + my_rank
    entry_group = jnp.arange(blocks * pick_count, dtype=jnp.int32) % pick_count // ROUNDS
    matched = (
        (owners_all[:, :, None] == my_index)
        & (ranks_all[:, :, None] == jnp.arange(slot_count, dtype=jnp.int32))
    ).astype(jnp.int32)
    send_block = jnp.sum(matched * locals_all[:, :, None], axis=1).reshape(-1)
    send_group = jnp.sum(matched * entry_group[None, :, None], axis=1).reshape(-1)
    send_live = jnp.sum(matched, axis=1).reshape(-1) > 0
    kv_grouped = kv_local.reshape(blocks, BLOCK, 2, groups, group_width)

    def pack_blocks():
        picked = kv_grouped[send_block, :, :, send_group, :]
        picked = jnp.where(send_live[:, None, None, None], picked, jnp.zeros((), picked.dtype))
        return picked.reshape(device_count, slot_count, BLOCK, 2, group_width)

    def unpack_blocks(arrived):
        arrived_flat = arrived.reshape(device_count * slot_count, BLOCK, 2, group_width)
        return arrived_flat[fetch_index].reshape(blocks, groups, ROUNDS, BLOCK, 2, group_width)

    random_kv = unpack_blocks(
        lax.all_to_all(pack_blocks(), "ctx", split_axis=0, concat_axis=0, tiled=True)
    )
    block_ids = jnp.arange(blocks)
    left_ok = jnp.logical_or(my_index > 0, block_ids > 0)
    right_ok = jnp.logical_or(my_index < device_count - 1, block_ids < blocks - 1)
    key_valid = jnp.concatenate(
        (
            jnp.repeat(left_ok[:, None], BLOCK, axis=1),
            jnp.ones((blocks, BLOCK), jnp.bool_),
            jnp.repeat(right_ok[:, None], BLOCK, axis=1),
            jnp.ones((blocks, (GLOBALS + ROUNDS) * BLOCK), jnp.bool_),
        ),
        axis=1,
    )
    valid_four = key_valid[:, None, None, :]

    def assemble(group_idx, source_kv):
        start_col = group_idx * group_width
        window = jnp.stack(
            [
                padded[offset : offset + blocks, :, :, start_col : start_col + group_width]
                for offset in range(3)
            ],
            axis=1,
        )
        global_part = jnp.broadcast_to(
            glob_kv[None, :, :, :, start_col : start_col + group_width],
            (blocks, GLOBALS, BLOCK, 2, group_width),
        )
        random_part = source_kv[:, group_idx]
        joined = jnp.concatenate((window, global_part, random_part), axis=1)
        joined = joined.reshape(blocks, key_span, 2, GROUP_HEADS, HEAD_DIM)
        return (joined[:, :, 0], joined[:, :, 1])

    def score_block(query_group, keys_group):
        scores = (
            jnp.einsum(
                "bqhd,bkhd->bhqk", query_group, keys_group, preferred_element_type=jnp.float32
            )
            * score_scale
        )
        return jnp.where(valid_four, scores, NEG_FILL)

    query_blocks = query.reshape(blocks, BLOCK, groups, GROUP_HEADS, HEAD_DIM)
    cot_blocks = cotangent.reshape(blocks, BLOCK, groups, GROUP_HEADS, HEAD_DIM)
    attended_parts = []
    totals = []
    for group_idx in range(groups):
        keys_group, vals_group = assemble(group_idx, random_kv)
        scores = score_block(query_blocks[:, :, group_idx], keys_group)
        row_max = jnp.max(scores, axis=-1, keepdims=True)
        weights = jnp.where(valid_four, jnp.exp(scores - row_max), 0.0)
        log_total = row_max + jnp.log(jnp.sum(weights, axis=-1, keepdims=True))
        probs_b = jnp.where(valid_four, jnp.exp(scores - log_total), 0.0).astype(jnp.bfloat16)
        attended_parts.append(
            jnp.einsum(
                "bhqk,bkhd->bqhd", probs_b, vals_group, preferred_element_type=jnp.float32
            ).astype(jnp.bfloat16)
        )
        totals.append(log_total)
    back_kv = unpack_blocks(
        lax.all_to_all(pack_blocks(), "ctx", split_axis=0, concat_axis=0, tiled=True)
    )
    win_acc = jnp.zeros((blocks + 2, BLOCK, 2, features), jnp.float32)
    glob_acc = jnp.zeros((GLOBALS, BLOCK, 2, features), jnp.float32)
    grad_query_parts = []
    random_terms = []
    for group_idx in range(groups):
        start_col = group_idx * group_width
        keys_group, vals_group = assemble(group_idx, back_kv)
        query_group = query_blocks[:, :, group_idx]
        cot_group = cot_blocks[:, :, group_idx]
        scores = score_block(query_group, keys_group)
        probs = jnp.where(valid_four, jnp.exp(scores - totals[group_idx]), 0.0)
        probs_b = probs.astype(jnp.bfloat16)
        row_dot = jnp.sum(
            cot_group.astype(jnp.float32) * attended_parts[group_idx].astype(jnp.float32), axis=-1
        )
        row_dot = jnp.transpose(row_dot, (0, 2, 1))[..., None]
        dprob = jnp.einsum(
            "bqhd,bkhd->bhqk", cot_group, vals_group, preferred_element_type=jnp.float32
        )
        dscore = (probs * (dprob - row_dot)).astype(jnp.bfloat16)
        grad_query_parts.append(
            (
                jnp.einsum(
                    "bhqk,bkhd->bqhd", dscore, keys_group, preferred_element_type=jnp.float32
                )
                * score_scale
            ).astype(jnp.bfloat16)
        )
        term_k = (
            jnp.einsum("bhqk,bqhd->bkhd", dscore, query_group, preferred_element_type=jnp.float32)
            * score_scale
        )
        term_v = jnp.einsum(
            "bhqk,bqhd->bkhd", probs_b, cot_group, preferred_element_type=jnp.float32
        )
        term_kv = jnp.stack((term_k, term_v), axis=2).reshape(
            blocks, key_kinds, BLOCK, 2, group_width
        )
        for offset in range(3):
            win_acc = win_acc.at[
                offset : offset + blocks, :, :, start_col : start_col + group_width
            ].add(term_kv[:, offset])
        glob_acc = glob_acc.at[:, :, :, start_col : start_col + group_width].add(
            jnp.sum(term_kv[:, 3 : 3 + GLOBALS], axis=0)
        )
        random_terms.append(term_kv[:, 3 + GLOBALS :].astype(jnp.bfloat16))
    random_flat = jnp.stack(random_terms, axis=1).reshape(
        blocks * pick_count, BLOCK, 2, group_width
    )
    grad_send = (
        jnp.zeros((device_count * slot_count, BLOCK, 2, group_width), jnp.bfloat16)
        .at[fetch_index]
        .set(random_flat)
    )
    grad_back = lax.all_to_all(
        grad_send.reshape(device_count, slot_count, BLOCK, 2, group_width),
        "ctx",
        split_axis=0,
        concat_axis=0,
        tiled=True,
    )
    grad_back = grad_back.reshape(device_count * slot_count, BLOCK, 2, group_width).astype(
        jnp.float32
    )
    grad_back = jnp.where(send_live[:, None, None, None], grad_back, 0.0)
    grad_owned = jnp.zeros((blocks, BLOCK, 2, groups, group_width), jnp.float32)
    grad_owned = grad_owned.at[send_block, :, :, send_group, :].add(grad_back)
    edge_sums = jnp.stack((win_acc[0], win_acc[blocks + 1]))
    edge_ext = padded_2(edge_sums, (("ctx", 0),), 1)
    glob_summed = lax.psum(glob_acc, "ctx")
    grad_total = win_acc[1 : blocks + 1] + grad_owned.reshape(blocks, BLOCK, 2, features)
    grad_total = grad_total.at[0].add(edge_ext[0]).at[blocks - 1].add(edge_ext[3])
    first_id = my_index * blocks + jnp.arange(blocks)
    for glob_index in range(GLOBALS):
        is_owner = global_ids[glob_index] == first_id
        grad_total = grad_total + jnp.where(
            is_owner[:, None, None, None], glob_summed[glob_index][None], 0.0
        )
    attended = jnp.stack(attended_parts, axis=2).reshape(tok_count, features)
    grad_query = jnp.stack(grad_query_parts, axis=2).reshape(tok_count, features)
    grad_key = grad_total[:, :, 0].reshape(tok_count, features).astype(jnp.bfloat16)
    grad_value = grad_total[:, :, 1].reshape(tok_count, features).astype(jnp.bfloat16)
    return (attended, grad_query, grad_key, grad_value)


def solution(mesh):
    return jax.shard_map(
        per_device,
        mesh=mesh,
        in_specs=(
            P(("groups", "ctx"), None),
            P(("groups", "ctx"), None),
            P(("groups", "ctx"), None),
            P(("groups", "ctx"), None),
            P("groups"),
            P("groups", None),
            P("groups", None),
        ),
        out_specs=(
            P(("groups", "ctx"), None),
            P(("groups", "ctx"), None),
            P(("groups", "ctx"), None),
            P(("groups", "ctx"), None),
        ),
        check_vma=False,
    )
```

profile of v0, /device:TPU:0, one launch (start us, length us, event | category | flops | bytes accessed | tf_op | source)
XLA Modules:
  0.0 544.2 jit_solution(3733437625669096891)
XLA Ops:
  15.0 4.5 broadcast_select_fusion
  19.4 7.6 %all-to-all-start = ((bf16[16,2,64,2,512]{4,2,3,1,0:T(8,128)(2,1)}), bf16[16,2,64,2,512]{4,2,3,1,0:T(8,128)(2,1)}, u32[]{:S(2)}, u32[]{:S(2)}) async-start(bf16[16,2,64,2,512]{4,2,3,1,0:T(8,128)(2,1)} %broadcast_select_fusion), calls=%async_computation | async-start | bytes 8388608 | tf_op jit(solution)/shard_map/all_to_all | solution.py:88
  50.0 130.4 %all-reduce.7.cloned.1.call-done = (bf16[1,64,2,1024]{3,1,2,0:T(8,128)(2,1)}, bf16[1,64,2,1024]{3,1,2,0:T(8,128)(2,1)}) async-done(((bf16[1,64,2,1024]{3,1,2,0:T(8,128)(2,1)}, bf16[1,64,2,1024]{3,1,2,0:T(8,128)(2,1)}), (bf16[1,64,2,1024]{3,1,2,0:T(8,128)(2,1)}, bf16[1,64,2,1024]{3,1,2,0:T(8,128)(2,1)})) %all-reduce.7.cloned.1.call-update) | async-done | bytes 524304 | tf_op jit(solution)/shard_map/psum | solution.py:29
  191.9 10.0 %copy.236 = bf16[4,8,64,2,512]{2,1,4,0,3:T(8,128)(2,1)} copy(bf16[4,8,64,2,512]{4,2,3,1,0:T(8,128)(2,1)} %get-tuple-element.138) | data formatting | bytes 8388608 | tf_op jit(solution)/shard_map/reshape | solution.py:119
  201.9 11.8 %reshape.691 = bf16[4,512,2,8,64]{1,4,3,0,2:T(8,128)(2,1)} reshape(bf16[4,8,64,2,512]{2,1,4,0,3:T(8,128)(2,1)} %copy.236) | data formatting | bytes 8388608 | tf_op jit(solution)/shard_map/reshape | solution.py:119
  213.7 10.0 %copy.234 = bf16[4,8,64,2,512]{2,1,4,0,3:T(8,128)(2,1)} copy(bf16[4,8,64,2,512]{4,2,3,1,0:T(8,128)(2,1)} %get-tuple-element.137) | data formatting | bytes 8388608 | tf_op jit(solution)/shard_map/reshape | solution.py:119
  223.8 11.8 %reshape.690 = bf16[4,512,2,8,64]{1,4,3,0,2:T(8,128)(2,1)} reshape(bf16[4,8,64,2,512]{2,1,4,0,3:T(8,128)(2,1)} %copy.234) | data formatting | bytes 8388608 | tf_op jit(solution)/shard_map/reshape | solution.py:119
  244.6 3.2 convolution_bitcast_fusion
  250.0 3.2 convolution_bitcast_fusion.1
  258.1 7.1 %reshape.688 = f32[4,8,64,1,512]{2,1,4,0,3:T(8,128)} reshape(f32[4,512,8,64]{1,3,2,0:T(8,128)} %convolution_bitcast_fusion) | data formatting | bytes 8388608 | tf_op jit(solution)/shard_map/stack | solution.py:186
  265.2 6.8 %copy.232 = f32[4,8,64,1,512]{4,2,1,0,3:T(8,128)} copy(f32[4,8,64,1,512]{2,1,4,0,3:T(8,128)} %reshape.688) | data formatting | bytes 8388608 | tf_op jit(solution)/shard_map/stack | solution.py:186
  274.7 7.1 %reshape.687 = f32[4,8,64,1,512]{2,1,4,0,3:T(8,128)} reshape(f32[4,512,8,64]{1,3,2,0:T(8,128)} %multiply_bitcast_fusion) | data formatting | bytes 8388608 | tf_op jit(solution)/shard_map/stack | solution.py:186
  281.8 6.8 %copy.231 = f32[4,8,64,1,512]{4,2,1,0,3:T(8,128)} copy(f32[4,8,64,1,512]{2,1,4,0,3:T(8,128)} %reshape.687) | data formatting | bytes 8388608 | tf_op jit(solution)/shard_map/stack | solution.py:186
  288.6 7.1 %reshape.686 = f32[4,8,64,1,512]{2,1,4,0,3:T(8,128)} reshape(f32[4,512,8,64]{1,3,2,0:T(8,128)} %convolution_bitcast_fusion.1) | data formatting | bytes 8388608 | tf_op jit(solution)/shard_map/stack | solution.py:186
  295.6 7.0 %copy.230 = f32[4,8,64,1,512]{4,2,1,0,3:T(8,128)} copy(f32[4,8,64,1,512]{2,1,4,0,3:T(8,128)} %reshape.686) | data formatting | bytes 8388608 | tf_op jit(solution)/shard_map/stack | solution.py:186
  305.3 7.1 %reshape.685 = f32[4,8,64,1,512]{2,1,4,0,3:T(8,128)} reshape(f32[4,512,8,64]{1,3,2,0:T(8,128)} %multiply_bitcast_fusion.1) | data formatting | bytes 8388608 | tf_op jit(solution)/shard_map/stack | solution.py:186
  312.4 6.9 %copy.229 = f32[4,8,64,1,512]{4,2,1,0,3:T(8,128)} copy(f32[4,8,64,1,512]{2,1,4,0,3:T(8,128)} %reshape.685) | data formatting | bytes 8388608 | tf_op jit(solution)/shard_map/stack | solution.py:186
  326.9 7.5 %scatter_fusion = bf16[32,64,2,512]{3,1,2,0:T(8,128)(2,1)} fusion(bf16[32,64,2,512]{3,1,2,0:T(8,128)(2,1)} %broadcast_in_dim.190, s32[24]{0:T(128)S(1)} %fusion.86, bf16[24,64,2,512]{3,1,2,0:T(8,128)(2,1)S(1)} %bitcast.294), kind=kCustom, calls=%fused_computation.2 | custom fusion | bytes 9437280 | tf_op jit(solution)/shard_map/scatter | solution.py:203
  334.5 5.4 all-to-all-start.1
  366.2 5.7 %scatter-add.41 = f32[6,64,2,1024]{3,1,0,2:T(8,128)S(1)} dynamic-update-slice(f32[6,64,2,1024]{3,1,0,2:T(8,128)S(1)} %fusion.58, f32[4,64,2,512]{3,1,0,2:T(8,128)} %add_select_fusion, s32[]{:T(128)} %bitcast.48, s32[]{:T(128)} %constant.374.clone.1, s32[]{:T(128)} %constant.374.clone.1, s32[]{:T(128)} %bitcast.49) | dynamic-update-slice | bytes 2097156 | tf_op jit(solution)/shard_map/scatter-add | solution.py:192
  386.9 115.4 %all-reduce.5.cloned.1.call-done = f32[2,64,2,1024]{3,1,0,2:T(8,128)} async-done(((f32[2,64,2,1024]{3,1,0,2:T(8,128)}), f32[2,64,2,1024]{3,1,0,2:T(8,128)}) %all-reduce.5.cloned.1.call-update) | async-done | bytes 1048592 | tf_op jit(solution)/shard_map/psum | solution.py:220
  504.6 6.9 %convert_select_fusion = f32[32,64,2,512]{3,1,2,0:T(8,128)} fusion(bf16[16,2,64,2,512]{4,2,3,1,0:T(8,128)(2,1)} %all-to-all-done.1, pred[32]{0:T(512)(128)(4,1)S(1)} %gt.20), kind=kLoop, calls=%fused_computation.20 | loop fusion | flops 4194304 | bytes 12582944 | tf_op jit(solution)/shard_map/jit(_where)/select_n | solution.py:215
  511.7 12.3 %scatter_fusion.1 = f32[4,64,2,2,512]{4,1,3,2,0:T(8,128)S(1)} fusion(f32[4,64,2,2,512]{4,1,3,2,0:T(8,128)S(1)} %broadcast_in_dim.188, s32[32]{0:T(128)S(1)} %get-tuple-element.133, f32[32,64,2,512]{3,1,2,0:T(8,128)} %convert_select_fusion), kind=kCustom, calls=%fused_computation.3 | custom fusion | flops 2097152 | bytes 25166080 | tf_op jit(solution)/shard_map/scatter-add | solution.py:217
  527.0 4.2 reshape.689
  (178 shorter events, 118.6 us)
Async XLA Ops:
  19.4 7.7 %copy-start.30 = (s32[2]{0:T(128)S(1)}, s32[2]{0:T(128)}, u32[]{:S(2)}) copy-start(s32[2]{0:T(128)} %param.31) | copy-start | bytes 28
  19.4 13.5 %copy-start.12 = (bf16[256,1024]{1,0:T(8,128)(2,1)S(1)}, bf16[256,1024]{1,0:T(8,128)(2,1)}, u32[]{:S(2)}) copy-start(bf16[256,1024]{1,0:T(8,128)(2,1)} %param.28) | copy-start | bytes 1572868
  19.4 13.5 %copy-start.13 = (bf16[256,1024]{1,0:T(8,128)(2,1)S(1)}, bf16[256,1024]{1,0:T(8,128)(2,1)}, u32[]{:S(2)}) copy-start(bf16[256,1024]{1,0:T(8,128)(2,1)} %param.29) | copy-start | bytes 1572868
  19.4 19.0 %copy-start.25 = (bf16[256,1024]{1,0:T(8,128)(2,1)S(1)}, bf16[256,1024]{1,0:T(8,128)(2,1)}, u32[]{:S(2)}) copy-start(bf16[256,1024]{1,0:T(8,128)(2,1)} %param.30) | copy-start | bytes 1572868
  19.4 167.6 %all-to-all-start = ((bf16[16,2,64,2,512]{4,2,3,1,0:T(8,128)(2,1)}), bf16[16,2,64,2,512]{4,2,3,1,0:T(8,128)(2,1)}, u32[]{:S(2)}, u32[]{:S(2)}) async-start(bf16[16,2,64,2,512]{4,2,3,1,0:T(8,128)(2,1)} %broadcast_select_fusion), calls=%async_computation | async-start | bytes 8388608 | tf_op jit(solution)/shard_map/all_to_all | solution.py:88
  27.1 153.4 %all-reduce.7.cloned.1.call-start = ((), (), s32[]{:S(2)}) async-start(), calls=%async_computation.3 | async-start | bytes 1048576 | tf_op jit(solution)/shard_map/psum | solution.py:29
  33.9 14.1 %collective-permute-start = (bf16[1,64,2,1024]{3,1,2,0:T(8,128)(2,1)}, bf16[1,64,2,1024]{3,1,2,0:T(8,128)(2,1)}, u32[]{:S(2)}, u32[]{:S(2)}) collective-permute-start(bf16[1,64,2,1024]{3,1,2,0:T(8,128)(2,1)} %get-tuple-element.154), channel_id=1, source_target_pairs={{0,1},{1,2},{2,3},{3,4},{4,5},{5,6},{6,7},{7,8},{8,9},{9,10},{10,1... | collective-permute-start | bytes 786440 | tf_op jit(solution)/shard_map/ppermute | solution.py:19
  36.9 146.6 %collective-permute-start.1 = (bf16[1,64,2,1024]{3,1,2,0:T(8,128)(2,1)S(1)}, bf16[1,64,2,1024]{3,1,2,0:T(8,128)(2,1)}, u32[]{:S(2)}, u32[]{:S(2)}) collective-permute-start(bf16[1,64,2,1024]{3,1,2,0:T(8,128)(2,1)S(1)} %get-tuple-element.155), channel_id=1, source_target_pairs={{1,0},{2,1},{3,2},{4,3},{5,4},{6,5},{7,6},{8,7},{9,8},{10,9},{11,1... | collective-permute-start | bytes 786440 | tf_op jit(solution)/shard_map/ppermute | solution.py:22
  223.7 11.8 %copy-start.18 = (bf16[4,64,1,8,64]{4,3,2,1,0:T(8,128)(2,1)S(1)}, bf16[4,64,1,8,64]{4,3,2,1,0:T(8,128)(2,1)}, u32[]{:S(2)}) copy-start(bf16[4,64,1,8,64]{4,3,2,1,0:T(8,128)(2,1)} %get-tuple-element.150) | copy-start | bytes 786436
  255.5 16.5 %copy-start.21 = (bf16[4,8,64,512]{3,2,1,0:T(8,128)(2,1)}, bf16[4,8,64,512]{3,2,1,0:T(8,128)(2,1)S(1)}, u32[]{:S(2)}) copy-start(bf16[4,8,64,512]{3,2,1,0:T(8,128)(2,1)S(1)} %fusion) | copy-start | bytes 6291460
  295.6 7.0 %copy-start.22 = (bf16[4,8,64,512]{3,2,1,0:T(8,128)(2,1)S(1)}, bf16[4,8,64,512]{3,2,1,0:T(8,128)(2,1)}, u32[]{:S(2)}) copy-start(bf16[4,8,64,512]{3,2,1,0:T(8,128)(2,1)} %fusion.1) | copy-start | bytes 6291460
  319.3 4.4 copy-start.7
  334.5 7.5 %copy-start.31 = (s32[4]{0:T(128)S(1)}, s32[4]{0:T(128)}, u32[]{:S(2)}) copy-start(s32[4]{0:T(128)} %constant.391.clone.1) | copy-start | bytes 52
  334.5 9.4 %copy-start.26 = (bf16[4,8,64,64]{3,2,1,0:T(8,128)(2,1)S(1)}, bf16[4,8,64,64]{3,2,1,0:T(8,128)(2,1)}, u32[]{:S(2)}) copy-start(bf16[4,8,64,64]{3,2,1,0:T(8,128)(2,1)} %get-tuple-element.165) | copy-start | bytes 786436
  334.5 9.4 %copy-start.27 = (bf16[4,8,64,64]{3,2,1,0:T(8,128)(2,1)S(1)}, bf16[4,8,64,64]{3,2,1,0:T(8,128)(2,1)}, u32[]{:S(2)}) copy-start(bf16[4,8,64,64]{3,2,1,0:T(8,128)(2,1)} %get-tuple-element.167) | copy-start | bytes 786436
  334.5 170.1 %all-to-all-start.1 = ((bf16[16,2,64,2,512]{4,2,3,1,0:T(8,128)(2,1)}), bf16[16,2,64,2,512]{4,2,3,1,0:T(8,128)(2,1)}, u32[]{:S(2)}, u32[]{:S(2)}) async-start(bf16[16,2,64,2,512]{4,2,3,1,0:T(8,128)(2,1)} %bitcast.283), calls=%async_computation.1 | async-start | bytes 8388608 | tf_op jit(solution)/shard_map/all_to_all | solution.py:205
  339.8 162.5 %all-reduce.5.cloned.1.call-start = ((), (), s32[]{:S(2)}) async-start(), calls=%async_computation.2 | async-start | bytes 2097152 | tf_op jit(solution)/shard_map/psum | solution.py:220
  371.9 4.1 copy-start.9
  381.4 130.1 %copy-start.10 = (f32[6,64,2,1024]{3,1,0,2:T(8,128)}, f32[6,64,2,1024]{3,1,0,2:T(8,128)S(1)}, u32[]{:S(2)}) copy-start(f32[6,64,2,1024]{3,1,0,2:T(8,128)S(1)} %fusion.48) | copy-start | bytes 9437188
  382.5 150.7 %collective-permute-start.2 = (f32[1,64,2,1024]{3,1,0,2:T(8,128)}, f32[1,64,2,1024]{3,1,0,2:T(8,128)}, u32[]{:S(2)}, u32[]{:S(2)}) collective-permute-start(f32[1,64,2,1024]{3,1,0,2:T(8,128)} %get-tuple-element.136), channel_id=1, source_target_pairs={{0,1},{1,2},{2,3},{3,4},{4,5},{5,6},{6,7},{7,8},{8,9},{9,10},{10,1... | collective-permute-start | bytes 1572872 | tf_op jit(solution)/shard_map/ppermute | solution.py:19
  385.6 148.8 %collective-permute-start.3 = (f32[1,64,2,1024]{3,1,0,2:T(8,128)}, f32[1,64,2,1024]{3,1,0,2:T(8,128)}, u32[]{:S(2)}, u32[]{:S(2)}) collective-permute-start(f32[1,64,2,1024]{3,1,0,2:T(8,128)} %get-tuple-element.135), channel_id=1, source_target_pairs={{1,0},{2,1},{3,2},{4,3},{5,4},{6,5},{7,6},{8,7},{9,8},{10,9},{11,1... | collective-permute-start | bytes 1572872 | tf_op jit(solution)/shard_map/ppermute | solution.py:22
  527.0 4.2 copy-start.11
  531.1 4.5 copy-start.23
  531.1 4.5 copy-start.24
  (16 other events, 47.2 us)
Sparse Core Ops, SparseCore 0:
  38.6 141.7 all-reduce.6
  377.4 124.8 all-reduce.4
where the time goes:
time: 550 us; the launch traced here: 544 us
  waiting for transfers between devices  246 us (45%)
  local copies, waits for them, and re-layouts  171 us (31%)
  other arithmetic  55 us (10%)
  matrix products  30.4 us (6%)
  starting transfers between devices  22 us (4%)
  between operations  20.1 us (4%)
    psum x1, waiting for transfers between devices, broadcast(): return lax.psum(jnp.where(mine, array, jnp.zeros_like(array)), axis)  130 us
    psum x1, waiting for transfers between devices, per_device(): glob_summed = lax.psum(glob_acc, 'ctx')  115 us
    another operation x8, local copies, waits for them, and re-layouts, per_device(): jnp.stack((term_k, term_v), axis=2)  55.7 us
    reshape x4, local copies, waits for them, and re-layouts, assemble(): joined = joined.reshape(blocks, key_span, 2, GROUP_HEADS, HEAD_DIM)  43.7 us
    unnamed x70, local copies, waits for them, and re-layouts  19.5 us
    scatter-add x1, other arithmetic, per_device(): grad_owned = grad_owned.at[send_block, :, :, send_group, :].add(grad_back)  12.3 us
  transfers between devices with their start and end apart: 8, of which 2 were waited for; matrix products, arithmetic and copies ran while one was open for 15% of the time, Pallas kernels for 0%

commit v1 on v0

--- a/solution.py
+++ b/solution.py
@@ -217,7 +217,7 @@
     grad_owned = grad_owned.at[send_block, :, :, send_group, :].add(grad_back)
     edge_sums = jnp.stack((win_acc[0], win_acc[blocks + 1]))
     edge_ext = padded_2(edge_sums, (("ctx", 0),), 1)
-    glob_summed = lax.psum(glob_acc, "ctx")
+    glob_summed = jnp.sum(lax.all_gather(glob_acc, "ctx"), axis=0)
     grad_total = win_acc[1 : blocks + 1] + grad_owned.reshape(blocks, BLOCK, 2, features)
     grad_total = grad_total.at[0].add(edge_ext[0]).at[blocks - 1].add(edge_ext[3])
     first_id = my_index * blocks + jnp.arange(blocks)

time: 550 us -> 585 us (1.064)
  the two profiles are of different devices: /device:TPU:0 before, /device:TPU:15 now
where the time goes in v1:
time: 585 us; the launch traced here: 579 us
  waiting for transfers between devices  267 us (46%)
  local copies, waits for them, and re-layouts  170 us (29%)
  other arithmetic  66.3 us (11%)
  matrix products  30.5 us (5%)
  starting transfers between devices  24.9 us (4%)
  between operations  19.7 us (3%)
    all_to_all x1, waiting for transfers between devices, per_device(): lax.all_to_all(grad_send.reshape(device_count, slot_count, BLOCK, 2, grou...  139 us
    ppermute x2, waiting for transfers between devices, padded_2(): lax.ppermute(lax.slice_in_dim(block, block.shape[dim] - width, None, axis...  75.9 us
    another operation x8, local copies, waits for them, and re-layouts, per_device(): jnp.stack((term_k, term_v), axis=2)  55.6 us
    psum x1, waiting for transfers between devices, broadcast(): return lax.psum(jnp.where(mine, array, jnp.zeros_like(array)), axis)  52.5 us
    reshape x4, local copies, waits for them, and re-layouts, assemble(): joined = joined.reshape(blocks, key_span, 2, GROUP_HEADS, HEAD_DIM)  43.8 us
    unnamed x66, local copies, waits for them, and re-layouts  19.5 us
    scatter-add x1, other arithmetic, per_device(): grad_owned = grad_owned.at[send_block, :, :, send_group, :].add(grad_back)  12.3 us
  transfers between devices with their start and end apart: 8, of which 3 were waited for; matrix products, arithmetic and copies ran while one was open for 17% of the time, Pallas kernels for 0%

profile of v1, /device:TPU:15, one launch (start us, length us, event | category | flops | bytes accessed | tf_op | source)
XLA Modules:
  0.0 578.7 jit_solution(12018558870932379248)
XLA Ops:
  15.0 4.5 broadcast_select_fusion
  19.4 6.7 %all-to-all-start = ((bf16[16,2,64,2,512]{4,2,3,1,0:T(8,128)(2,1)}), bf16[16,2,64,2,512]{4,2,3,1,0:T(8,128)(2,1)}, u32[]{:S(2)}, u32[]{:S(2)}) async-start(bf16[16,2,64,2,512]{4,2,3,1,0:T(8,128)(2,1)} %broadcast_select_fusion), calls=%async_computation | async-start | bytes 8388608 | tf_op jit(solution)/shard_map/all_to_all | solution.py:88
  47.7 75.9 %collective-permute-done = bf16[1,64,2,1024]{3,1,2,0:T(8,128)(2,1)} collective-permute-done((bf16[1,64,2,1024]{3,1,2,0:T(8,128)(2,1)}, bf16[1,64,2,1024]{3,1,2,0:T(8,128)(2,1)}, u32[]{:S(2)}, u32[]{:S(2)}) %collective-permute-start) | collective-permute-done | bytes 262176 | tf_op jit(solution)/shard_map/ppermute | solution.py:19
  125.7 52.5 %all-reduce.5.cloned.1.call-done = (bf16[1,64,2,1024]{3,1,2,0:T(8,128)(2,1)}, bf16[1,64,2,1024]{3,1,2,0:T(8,128)(2,1)}) async-done(((bf16[1,64,2,1024]{3,1,2,0:T(8,128)(2,1)}, bf16[1,64,2,1024]{3,1,2,0:T(8,128)(2,1)}), (bf16[1,64,2,1024]{3,1,2,0:T(8,128)(2,1)}, bf16[1,64,2,1024]{3,1,2,0:T(8,128)(2,1)})) %all-reduce.5.cloned.1.call-update) | async-done | bytes 524304 | tf_op jit(solution)/shard_map/psum | solution.py:29
  189.7 10.0 %copy.239 = bf16[4,8,64,2,512]{2,1,4,0,3:T(8,128)(2,1)} copy(bf16[4,8,64,2,512]{4,2,3,1,0:T(8,128)(2,1)} %get-tuple-element.138) | data formatting | bytes 8388608 | tf_op jit(solution)/shard_map/reshape | solution.py:119
  199.7 11.8 %reshape.693 = bf16[4,512,2,8,64]{1,4,3,0,2:T(8,128)(2,1)} reshape(bf16[4,8,64,2,512]{2,1,4,0,3:T(8,128)(2,1)} %copy.239) | data formatting | bytes 8388608 | tf_op jit(solution)/shard_map/reshape | solution.py:119
  211.5 10.0 %copy.237 = bf16[4,8,64,2,512]{2,1,4,0,3:T(8,128)(2,1)} copy(bf16[4,8,64,2,512]{4,2,3,1,0:T(8,128)(2,1)} %get-tuple-element.137) | data formatting | bytes 8388608 | tf_op jit(solution)/shard_map/reshape | solution.py:119
  221.5 11.9 %reshape.692 = bf16[4,512,2,8,64]{1,4,3,0,2:T(8,128)(2,1)} reshape(bf16[4,8,64,2,512]{2,1,4,0,3:T(8,128)(2,1)} %copy.237) | data formatting | bytes 8388608 | tf_op jit(solution)/shard_map/reshape | solution.py:119
  256.0 7.1 %reshape.690 = f32[4,8,64,1,512]{2,1,4,0,3:T(8,128)} reshape(f32[4,512,8,64]{1,3,2,0:T(8,128)} %convolution_bitcast_fusion) | data formatting | bytes 8388608 | tf_op jit(solution)/shard_map/stack | solution.py:186
  263.1 6.8 %copy.235 = f32[4,8,64,1,512]{4,2,1,0,3:T(8,128)} copy(f32[4,8,64,1,512]{2,1,4,0,3:T(8,128)} %reshape.690) | data formatting | bytes 8388608 | tf_op jit(solution)/shard_map/stack | solution.py:186
  272.6 7.1 %reshape.689 = f32[4,8,64,1,512]{2,1,4,0,3:T(8,128)} reshape(f32[4,512,8,64]{1,3,2,0:T(8,128)} %multiply_bitcast_fusion) | data formatting | bytes 8388608 | tf_op jit(solution)/shard_map/stack | solution.py:186
  279.7 6.8 %copy.234 = f32[4,8,64,1,512]{4,2,1,0,3:T(8,128)} copy(f32[4,8,64,1,512]{2,1,4,0,3:T(8,128)} %reshape.689) | data formatting | bytes 8388608 | tf_op jit(solution)/shard_map/stack | solution.py:186
  286.5 7.1 %reshape.688 = f32[4,8,64,1,512]{2,1,4,0,3:T(8,128)} reshape(f32[4,512,8,64]{1,3,2,0:T(8,128)} %convolution_bitcast_fusion.1) | data formatting | bytes 8388608 | tf_op jit(solution)/shard_map/stack | solution.py:186
  293.5 7.0 %copy.233 = f32[4,8,64,1,512]{4,2,1,0,3:T(8,128)} copy(f32[4,8,64,1,512]{2,1,4,0,3:T(8,128)} %reshape.688) | data formatting | bytes 8388608 | tf_op jit(solution)/shard_map/stack | solution.py:186
  303.3 7.1 %reshape.687 = f32[4,8,64,1,512]{2,1,4,0,3:T(8,128)} reshape(f32[4,512,8,64]{1,3,2,0:T(8,128)} %multiply_bitcast_fusion.1) | data formatting | bytes 8388608 | tf_op jit(solution)/shard_map/stack | solution.py:186
  310.4 6.8 %copy.232 = f32[4,8,64,1,512]{4,2,1,0,3:T(8,128)} copy(f32[4,8,64,1,512]{2,1,4,0,3:T(8,128)} %reshape.687) | data formatting | bytes 8388608 | tf_op jit(solution)/shard_map/stack | solution.py:186
  330.3 7.8 %scatter_fusion = bf16[32,64,2,512]{3,1,2,0:T(8,128)(2,1)} fusion(bf16[32,64,2,512]{3,1,2,0:T(8,128)(2,1)} %broadcast_in_dim.190, s32[24]{0:T(128)S(1)} %fusion.86, bf16[24,64,2,512]{3,1,2,0:T(8,128)(2,1)S(1)} %bitcast.298), kind=kCustom, calls=%fused_computation.2 | custom fusion | bytes 9437280 | tf_op jit(solution)/shard_map/scatter | solution.py:203
  338.1 7.4 %all-to-all-start.1 = ((bf16[16,2,64,2,512]{4,2,3,1,0:T(8,128)(2,1)}), bf16[16,2,64,2,512]{4,2,3,1,0:T(8,128)(2,1)}, u32[]{:S(2)}, u32[]{:S(2)}) async-start(bf16[16,2,64,2,512]{4,2,3,1,0:T(8,128)(2,1)} %bitcast.287), calls=%async_computation.1 | async-start | bytes 8388608 | tf_op jit(solution)/shard_map/all_to_all | solution.py:205
  371.5 5.6 scatter-add.45
  387.7 139.0 %all-to-all-done.1 = bf16[16,2,64,2,512]{4,2,3,1,0:T(8,128)(2,1)} async-done(((bf16[16,2,64,2,512]{4,2,3,1,0:T(8,128)(2,1)}), bf16[16,2,64,2,512]{4,2,3,1,0:T(8,128)(2,1)}, u32[]{:S(2)}, u32[]{:S(2)}) %all-to-all-start.1) | async-done | bytes 4194336 | tf_op jit(solution)/shard_map/all_to_all | solution.py:205
  526.7 6.8 %convert_select_fusion = f32[32,64,2,512]{3,1,2,0:T(8,128)} fusion(bf16[16,2,64,2,512]{4,2,3,1,0:T(8,128)(2,1)} %all-to-all-done.1, pred[32]{0:T(512)(128)(4,1)S(1)} %gt.20), kind=kLoop, calls=%fused_computation.20 | loop fusion | flops 4194304 | bytes 12582944 | tf_op jit(solution)/shard_map/jit(_where)/select_n | solution.py:215
  533.8 12.3 %scatter_fusion.1 = f32[4,64,2,2,512]{4,1,3,2,0:T(8,128)S(1)} fusion(f32[4,64,2,2,512]{4,1,3,2,0:T(8,128)S(1)} %broadcast_in_dim.188, s32[32]{0:T(128)S(1)} %get-tuple-element.133, f32[32,64,2,512]{3,1,2,0:T(8,128)} %convert_select_fusion), kind=kCustom, calls=%fused_computation.3 | custom fusion | flops 2097152 | bytes 25166080 | tf_op jit(solution)/shard_map/scatter-add | solution.py:217
  549.1 4.2 reshape.691
  560.7 7.8 %reduce_sum.109 = f32[2,64,2,1024]{3,1,2,0:T(8,128)S(1)} reduce(f32[16,2,64,2,1024]{4,2,3,1,0:T(8,128)} %all-gather.2.cloned.1.call-done, f32[]{:T(128)} %constant.389.clone.1), dimensions={0}, to_apply=%region_18.19 | reduce | flops 3932160 | bytes 17825796 | tf_op jit(solution)/shard_map/reduce_sum | solution.py:220
  (177 shorter events, 129.3 us)
Async XLA Ops:
  7.2 4.0 copy-start.27
  19.4 6.7 %copy-start.28 = (s32[2]{0:T(128)S(1)}, s32[2]{0:T(128)}, u32[]{:S(2)}) copy-start(s32[2]{0:T(128)} %param.31) | copy-start | bytes 28
  19.4 12.1 %copy-start.12 = (bf16[256,1024]{1,0:T(8,128)(2,1)S(1)}, bf16[256,1024]{1,0:T(8,128)(2,1)}, u32[]{:S(2)}) copy-start(bf16[256,1024]{1,0:T(8,128)(2,1)} %param.28) | copy-start | bytes 1572868
  19.4 12.1 %copy-start.13 = (bf16[256,1024]{1,0:T(8,128)(2,1)S(1)}, bf16[256,1024]{1,0:T(8,128)(2,1)}, u32[]{:S(2)}) copy-start(bf16[256,1024]{1,0:T(8,128)(2,1)} %param.29) | copy-start | bytes 1572868
  19.4 18.7 %copy-start.23 = (bf16[256,1024]{1,0:T(8,128)(2,1)S(1)}, bf16[256,1024]{1,0:T(8,128)(2,1)}, u32[]{:S(2)}) copy-start(bf16[256,1024]{1,0:T(8,128)(2,1)} %param.30) | copy-start | bytes 1572868
  19.4 165.4 %all-to-all-start = ((bf16[16,2,64,2,512]{4,2,3,1,0:T(8,128)(2,1)}), bf16[16,2,64,2,512]{4,2,3,1,0:T(8,128)(2,1)}, u32[]{:S(2)}, u32[]{:S(2)}) async-start(bf16[16,2,64,2,512]{4,2,3,1,0:T(8,128)(2,1)} %broadcast_select_fusion), calls=%async_computation | async-start | bytes 8388608 | tf_op jit(solution)/shard_map/all_to_all | solution.py:88
  26.1 152.0 %all-reduce.5.cloned.1.call-start = ((), (), s32[]{:S(2)}) async-start(), calls=%async_computation.3 | async-start | bytes 1048576 | tf_op jit(solution)/shard_map/psum | solution.py:29
  32.5 91.1 %collective-permute-start = (bf16[1,64,2,1024]{3,1,2,0:T(8,128)(2,1)}, bf16[1,64,2,1024]{3,1,2,0:T(8,128)(2,1)}, u32[]{:S(2)}, u32[]{:S(2)}) collective-permute-start(bf16[1,64,2,1024]{3,1,2,0:T(8,128)(2,1)} %get-tuple-element.154), channel_id=1, source_target_pairs={{0,1},{1,2},{2,3},{3,4},{4,5},{5,6},{6,7},{7,8},{8,9},{9,10},{10,1... | collective-permute-start | bytes 786440 | tf_op jit(solution)/shard_map/ppermute | solution.py:19
  35.8 145.3 %collective-permute-start.1 = (bf16[1,64,2,1024]{3,1,2,0:T(8,128)(2,1)S(1)}, bf16[1,64,2,1024]{3,1,2,0:T(8,128)(2,1)}, u32[]{:S(2)}, u32[]{:S(2)}) collective-permute-start(bf16[1,64,2,1024]{3,1,2,0:T(8,128)(2,1)S(1)} %get-tuple-element.155), channel_id=1, source_target_pairs={{1,0},{2,1},{3,2},{4,3},{5,4},{6,5},{7,6},{8,7},{9,8},{10,9},{11,1... | collective-permute-start | bytes 786440 | tf_op jit(solution)/shard_map/ppermute | solution.py:22
  37.8 522.9 %all-gather.2.cloned.1.call-start = ((), (), s32[]{:S(2)}) async-start(), calls=%async_computation.2 | async-start | bytes 17825792 | tf_op jit(solution)/shard_map/all_gather | solution.py:220
  221.5 11.9 %copy-start.18 = (bf16[4,64,1,8,64]{4,3,2,1,0:T(8,128)(2,1)S(1)}, bf16[4,64,1,8,64]{4,3,2,1,0:T(8,128)(2,1)}, u32[]{:S(2)}) copy-start(bf16[4,64,1,8,64]{4,3,2,1,0:T(8,128)(2,1)} %get-tuple-element.150) | copy-start | bytes 786436
  253.3 16.6 %copy-start.21 = (bf16[4,8,64,512]{3,2,1,0:T(8,128)(2,1)}, bf16[4,8,64,512]{3,2,1,0:T(8,128)(2,1)S(1)}, u32[]{:S(2)}) copy-start(bf16[4,8,64,512]{3,2,1,0:T(8,128)(2,1)S(1)} %fusion) | copy-start | bytes 6291460
  293.5 7.0 %copy-start.22 = (bf16[4,8,64,512]{3,2,1,0:T(8,128)(2,1)S(1)}, bf16[4,8,64,512]{3,2,1,0:T(8,128)(2,1)}, u32[]{:S(2)}) copy-start(bf16[4,8,64,512]{3,2,1,0:T(8,128)(2,1)} %fusion.1) | copy-start | bytes 6291460
  317.2 4.1 copy-start.3
  322.7 4.4 copy-start.8
  338.1 9.2 %copy-start.29 = (s32[4]{0:T(128)S(1)}, s32[4]{0:T(128)}, u32[]{:S(2)}) copy-start(s32[4]{0:T(128)} %constant.392.clone.1) | copy-start | bytes 52
  338.1 11.2 %copy-start.24 = (bf16[4,8,64,64]{3,2,1,0:T(8,128)(2,1)S(1)}, bf16[4,8,64,64]{3,2,1,0:T(8,128)(2,1)}, u32[]{:S(2)}) copy-start(bf16[4,8,64,64]{3,2,1,0:T(8,128)(2,1)} %get-tuple-element.165) | copy-start | bytes 786436
  338.1 11.2 %copy-start.25 = (bf16[4,8,64,64]{3,2,1,0:T(8,128)(2,1)S(1)}, bf16[4,8,64,64]{3,2,1,0:T(8,128)(2,1)}, u32[]{:S(2)}) copy-start(bf16[4,8,64,64]{3,2,1,0:T(8,128)(2,1)} %get-tuple-element.167) | copy-start | bytes 786436
  338.1 188.6 %all-to-all-start.1 = ((bf16[16,2,64,2,512]{4,2,3,1,0:T(8,128)(2,1)}), bf16[16,2,64,2,512]{4,2,3,1,0:T(8,128)(2,1)}, u32[]{:S(2)}, u32[]{:S(2)}) async-start(bf16[16,2,64,2,512]{4,2,3,1,0:T(8,128)(2,1)} %bitcast.287), calls=%async_computation.1 | async-start | bytes 8388608 | tf_op jit(solution)/shard_map/all_to_all | solution.py:205
  377.2 3.8 copy-start.5
  381.3 152.3 %copy-start.10 = (f32[6,64,2,1024]{3,1,0,2:T(8,128)}, f32[6,64,2,1024]{3,1,0,2:T(8,128)S(1)}, u32[]{:S(2)}) copy-start(f32[6,64,2,1024]{3,1,0,2:T(8,128)S(1)} %fusion.48) | copy-start | bytes 9437188
  382.5 174.1 %collective-permute-start.2 = (f32[1,64,2,1024]{3,1,0,2:T(8,128)}, f32[1,64,2,1024]{3,1,0,2:T(8,128)}, u32[]{:S(2)}, u32[]{:S(2)}) collective-permute-start(f32[1,64,2,1024]{3,1,0,2:T(8,128)} %get-tuple-element.136), channel_id=1, source_target_pairs={{0,1},{1,2},{2,3},{3,4},{4,5},{5,6},{6,7},{7,8},{8,9},{9,10},{10,1... | collective-permute-start | bytes 1572872 | tf_op jit(solution)/shard_map/ppermute | solution.py:19
  385.8 172.8 %collective-permute-start.3 = (f32[1,64,2,1024]{3,1,0,2:T(8,128)}, f32[1,64,2,1024]{3,1,0,2:T(8,128)}, u32[]{:S(2)}, u32[]{:S(2)}) collective-permute-start(f32[1,64,2,1024]{3,1,0,2:T(8,128)} %get-tuple-element.135), channel_id=1, source_target_pairs={{1,0},{2,1},{3,2},{4,3},{5,4},{6,5},{7,6},{8,7},{9,8},{10,9},{11,1... | collective-permute-start | bytes 1572872 | tf_op jit(solution)/shard_map/ppermute | solution.py:22
  549.1 4.2 copy-start.11
  (14 other events, 39.5 us)
Sparse Core Ops, SparseCore 0:
  37.9 140.1 all-reduce.4
  322.8 205.6 all-gather.1
